TPU v7x, 32 devices: a whole 2x2x4 slice. The times are simulated.
32 devices in a mesh: tensor: 4 (over z), example: 8 (over y, x, core).
Axes of the slice: x: 2, y: 2, z: 4, core: 2. Of those that a mesh axis runs over, the one named last changes fastest.
Arguments:
- queries: bfloat16 [1, 4096, 4096], P(None, 'example', 'tensor'), may hold values from -0.0014648438 to 0.0014648438
- basis_out: bfloat16 [4096, 4096], P('example', 'tensor'), may hold values from -0.09375 to 0.09375
- basis_in: bfloat16 [4096, 4096], P('tensor', 'example'), may hold values from -0.09375 to 0.09375
- eigvals: float32 [4096, 4096], P('tensor', 'example'), may hold values from 0.25 to 4
- input_fac: bfloat16 [128, 8, 4096], P('example', None, 'tensor'), may hold values from -6 to 6
- grad_fac: bfloat16 [128, 8, 4096], P('example', None, 'tensor'), may hold values from -6 to 6
- cand_slot: int32 [128], replicated, may hold values from 0 to 127, as said below
- score_list: int32 [8, 16], replicated, may hold values from 0 to 127, as said below
- token_count: int32 [128], replicated, may hold values from 1 to 8
Outputs:
- scores: float32 [1, 128, 8], P(None, 'example')
Inputs may be any that keep to these rules, and one draw needn't show every extreme that they name: `cand_slot`: a permutation; slot s belongs to owner s // 16. `score_list`: every candidate appears exactly once; a scorer's list holds at most 4 candidates of any one owner, and some scorer takes exactly 4 from some owner.
All inputs are finite; a program needn't handle non-finite values.
Results may differ from a plain program's by a relative error of at most 0.019.
Values may be sent and summed in bfloat16 or wider, within the bound.
A program may use at most 128 MiB of HBM per device.

v0:
```python
import jax
import jax.numpy as jnp
from jax import lax
from jax.sharding import PartitionSpec as P


def body(
    queries, basis_out, basis_in, eigvals, input_fac, grad_fac, cand_slot, score_list, token_count
):
    ex_count = lax.axis_size("example")
    my_index = lax.axis_index("example")
    out_rows = lax.all_gather(basis_out, "tensor", axis=1, tiled=True)
    in_rows = lax.all_gather(basis_in, "example", axis=1, tiled=True)
    query_total = queries.shape[0]
    columns = out_rows
    rotated = lax.psum_scatter(
        jnp.einsum("ki,qkj->iqj", columns, queries, preferred_element_type=jnp.float32).astype(
            jnp.bfloat16
        ),
        "example",
        scatter_dimension=0,
        tiled=True,
    )
    columns = in_rows
    core_sum = lax.psum_scatter(
        jnp.einsum("kj,iqk->jqi", columns, rotated, preferred_element_type=jnp.float32).astype(
            jnp.bfloat16
        ),
        "tensor",
        scatter_dimension=0,
        tiled=True,
    ).astype(jnp.float32)
    scaled = (core_sum / eigvals[:, None, :]).astype(jnp.bfloat16)
    columns = out_rows
    turned = jnp.einsum(
        "jqk,ik->jqi",
        lax.all_gather(scaled, "example", axis=2, tiled=True),
        columns,
        preferred_element_type=jnp.float32,
    ).astype(jnp.bfloat16)
    columns = in_rows
    precond = jnp.einsum(
        "jk,kqi->jqi",
        columns,
        lax.all_gather(turned, "tensor", axis=0, tiled=True),
        preferred_element_type=jnp.float32,
    ).astype(jnp.bfloat16)
    cand_total = cand_slot.shape[0]
    cand_dev = input_fac.shape[0]
    token_len = input_fac.shape[1]
    shard_width = input_fac.shape[2]
    list_len = score_list.shape[1]
    cand_ids = jnp.arange(cand_total, dtype=jnp.int32)
    matches = (score_list[:, :, None] == cand_ids[None, None, :]).astype(jnp.int32)
    entry_slot = jnp.sum(matches * cand_slot[None, None, :], axis=2)
    entry_count = jnp.sum(matches * token_count[None, None, :], axis=2)
    entry_owner = entry_slot // cand_dev
    entry_local = entry_slot % cand_dev
    earlier = jnp.arange(list_len)[:, None] > jnp.arange(list_len)[None, :]
    same_owner = entry_owner[:, :, None] == entry_owner[:, None, :]
    entry_rank = jnp.sum((same_owner & earlier[None]).astype(jnp.int32), axis=2)
    capacity = 2 * cand_dev // ex_count
    place_ids = jnp.arange(capacity, dtype=jnp.int32)
    local_ids = jnp.arange(cand_dev, dtype=jnp.int32)
    owned_here = entry_owner == my_index
    send_table = jnp.sum(
        (
            owned_here[:, :, None, None]
            & (entry_rank[:, :, None, None] == place_ids[None, None, :, None])
            & (entry_local[:, :, None, None] == local_ids[None, None, None, :])
        ).astype(jnp.float32),
        axis=1,
    )
    my_owner = lax.dynamic_index_in_dim(entry_owner, my_index, 0, keepdims=False)
    my_rank = lax.dynamic_index_in_dim(entry_rank, my_index, 0, keepdims=False)
    my_count = lax.dynamic_index_in_dim(entry_count, my_index, 0, keepdims=False)
    source_ids = jnp.arange(ex_count, dtype=jnp.int32)
    take_table = (
        (
            (my_owner[:, None, None] == source_ids[None, :, None])
            & (my_rank[:, None, None] == place_ids[None, None, :])
        )
        .astype(jnp.float32)
        .reshape(list_len, ex_count * capacity)
    )
    select_send = send_table.astype(jnp.bfloat16)
    select_take = take_table.astype(jnp.bfloat16)

    def route_rows(owned_rows):
        return jnp.einsum(
            "ers,sx->erx", select_send, owned_rows, preferred_element_type=jnp.float32
        ).astype(jnp.bfloat16)

    def collect_rows(received):
        flat_received = received.reshape(ex_count * capacity, received.shape[2])
        return jnp.dot(select_take, flat_received, preferred_element_type=jnp.float32).astype(
            jnp.bfloat16
        )

    flat_acts = input_fac.reshape(cand_dev, token_len * shard_width)
    flat_grads = grad_fac.reshape(cand_dev, token_len * shard_width)
    sent_acts, sent_grads = (
        lax.all_to_all(route_rows(flat_acts), "example", split_axis=0, concat_axis=0, tiled=True),
        lax.all_to_all(route_rows(flat_grads), "example", split_axis=0, concat_axis=0, tiled=True),
    )
    got_acts = collect_rows(sent_acts).reshape(list_len * token_len, shard_width)
    got_grads = collect_rows(sent_grads).reshape(list_len * token_len, shard_width)
    whole_grads = lax.all_gather(got_grads, "tensor", axis=1, tiled=True)
    columns = whole_grads
    weighted = jnp.einsum(
        "tn,jqn->qtj",
        columns,
        lax.all_gather(precond, "example", axis=2, tiled=True),
        preferred_element_type=jnp.float32,
    )
    partial_scores = jnp.sum(got_acts.astype(jnp.float32)[None] * weighted, axis=2)
    summed = lax.psum(partial_scores, "tensor").reshape(query_total, list_len, token_len)
    live_mask = jnp.arange(token_len, dtype=jnp.int32)[None, :] < my_count[:, None]
    return jnp.where(live_mask[None], summed, jnp.float32(0.0))


def solution(mesh):
    in_specs = (
        P(None, "example", "tensor"),
        P("example", "tensor"),
        P("tensor", "example"),
        P("tensor", "example"),
        P("example", None, "tensor"),
        P("example", None, "tensor"),
        P(),
        P(),
        P(),
    )
    out_specs = P(None, "example", None)
    return jax.shard_map(body, mesh=mesh, in_specs=in_specs, out_specs=out_specs, check_vma=False)
```

profile of v0, /device:TPU:0, one launch (start us, length us, event | category | flops | bytes accessed | tf_op | source)
XLA Modules:
  0.0 568.8 jit_solution(2000959011714621672)
XLA Ops:
  6.5 0.0 copy-start
  6.5 0.0 all-gather.9.cloned.1.call-start
  6.5 0.7 all-gather.9.cloned.1.call-update
  7.3 0.0 all-gather.11.cloned.1.call-start
  7.3 0.7 all-gather.11.cloned.1.call-update
  8.0 0.0 reduce-scatter.3.cloned.1.call-start
  8.1 84.4 %all-gather.9.cloned.1.call-done = bf16[512,4096]{1,0:T(8,128)(2,1)} async-done(((bf16[512,1024]{1,0:T(8,128)(2,1)}), bf16[512,4096]{1,0:T(8,128)(2,1)}) %all-gather.9.cloned.1.call-update) | async-done | bytes 4194320 | tf_op jit(solution)/shard_map/all_gather | solution.py:12
  92.4 0.0 copy-done
  92.4 9.0 %convert_bitcast_fusion = bf16[4096,1,1024]{2,0,1:T(8,128)(2,1)} fusion(bf16[512,4096]{1,0:T(8,128)(2,1)} %all-gather.9.cloned.1.call-done, bf16[1,512,1024]{2,1,0:T(8,128)(2,1)S(1)} %copy-done), kind=kOutput, calls=%fused_computation.9 | convolution fusion | flops 4299161600 | bytes 13631488 | tf_op jit(solution)/shard_map/ki,qkj->iqj/dot_general | solution.py:17
  101.4 0.0 reduce-scatter.3.cloned.1.call-update
  101.4 0.0 reduce-scatter.5.cloned.1.call-start
  101.5 47.3 %all-gather.11.cloned.1.call-done = bf16[1024,4096]{1,0:T(8,128)(2,1)} async-done(((bf16[1024,512]{1,0:T(8,128)(2,1)}), bf16[1024,4096]{1,0:T(8,128)(2,1)}) %all-gather.11.cloned.1.call-update) | async-done | bytes 8388624 | tf_op jit(solution)/shard_map/all_gather | solution.py:13
  148.8 74.8 %reduce-scatter.3.cloned.1.call-done = bf16[512,1,1024]{2,0,1:T(8,128)(2,1)} async-done(((bf16[4096,1,1024]{2,0,1:T(8,128)(2,1)}), bf16[512,1,1024]{2,0,1:T(8,128)(2,1)}) %reduce-scatter.3.cloned.1.call-update) | async-done | bytes 1048592 | tf_op jit(solution)/shard_map/reduce_scatter | solution.py:16
  223.6 10.2 %fusion.5 = bf16[4096,1,512]{0,2,1:T(8,128)(2,1)} fusion(bf16[1024,4096]{1,0:T(8,128)(2,1)} %all-gather.11.cloned.1.call-done, bf16[512,1,1024]{2,0,1:T(8,128)(2,1)} %reduce-scatter.3.cloned.1.call-done), kind=kOutput, calls=%fused_computation.11 | convolution fusion | flops 4297064448 | bytes 13631488 | tf_op jit(solution)/shard_map/kj,iqk->jqi/dot_general | solution.py:26
  233.8 0.0 reduce-scatter.5.cloned.1.call-update
  233.8 0.0 all-gather.13.cloned.1.call-start
  233.9 1.9 copy.26
  235.8 74.9 %reduce-scatter.5.cloned.1.call-done = bf16[1024,1,512]{0,2,1:T(8,128)(2,1)} async-done(((bf16[4096,1,512]{0,2,1:T(8,128)(2,1)}), bf16[1024,1,512]{0,2,1:T(8,128)(2,1)}) %reduce-scatter.5.cloned.1.call-update) | async-done | bytes 1048592 | tf_op jit(solution)/shard_map/reduce_scatter | solution.py:25
  310.7 2.6 fusion.6
  313.3 0.0 all-gather.13.cloned.1.call-update
  313.4 0.0 copy-start.1
  313.4 0.0 copy-start.3
  313.4 0.0 copy-start.4
  313.4 0.0 copy-start.5
  313.4 0.2 all-gather.17.cloned.1.call-start
  313.6 54.8 %all-gather.13.cloned.1.call-done = bf16[1024,1,4096]{0,2,1:T(8,128)(2,1)} async-done(((bf16[1024,1,512]{0,2,1:T(8,128)(2,1)}), bf16[1024,1,4096]{0,2,1:T(8,128)(2,1)}) %all-gather.13.cloned.1.call-update) | async-done | bytes 8388624 | tf_op jit(solution)/shard_map/all_gather | solution.py:37
  368.4 10.1 %fusion.7 = bf16[1024,512]{1,0:T(8,128)(2,1)} fusion(bf16[512,4096]{1,0:T(8,128)(2,1)} %all-gather.9.cloned.1.call-done, bf16[1024,1,4096]{0,2,1:T(8,128)(2,1)} %all-gather.13.cloned.1.call-done), kind=kOutput, calls=%fused_computation.14 | convolution fusion | flops 4295491584 | bytes 13631488 | tf_op jit(solution)/shard_map/jqk,ik->jqi/dot_general | solution.py:35
  378.5 0.0 all-gather.17.cloned.1.call-update
  378.5 0.0 copy-done.1
  378.5 0.1 reshape.275
  378.7 0.0 copy-done.3
  378.7 0.0 copy-done.4
  378.7 0.4 select_reduce_fusion.1
  379.1 0.3 convert_reduce_fusion.1
  379.5 0.1 iota_compare_fusion
  379.5 0.2 convert_reduce_fusion
  379.7 0.3 convolution_convert_fusion
  380.0 1.2 copy.28
  381.2 3.5 all-to-all-start.1
  384.7 0.0 all-gather.15.cloned.1.call-start
  384.8 9.6 %all-to-all-done.1 = bf16[8,4,8192]{2,1,0:T(4,128)(2,1)S(1)} async-done(((bf16[8,4,8192]{2,1,0:T(4,128)(2,1)}), bf16[8,4,8192]{2,1,0:T(4,128)(2,1)S(1)}, u32[]{:S(2)}, u32[]{:S(2)}) %all-to-all-start.1) | async-done | bytes 524320 | tf_op jit(solution)/shard_map/all_to_all | solution.py:104
  394.4 0.4 fusion.2
  394.8 0.9 reshape.265
  395.6 0.0 all-gather.15.cloned.1.call-update
  395.7 0.0 copy-start.2
  395.7 0.3 all-gather.19.cloned.1.call-start
  396.0 63.5 %all-gather.17.cloned.1.call-done = bf16[4096,512]{1,0:T(8,128)(2,1)} async-done(((bf16[1024,512]{1,0:T(8,128)(2,1)}), bf16[4096,512]{1,0:T(8,128)(2,1)}) %all-gather.17.cloned.1.call-update) | async-done | bytes 4194320 | tf_op jit(solution)/shard_map/all_gather | solution.py:45
  459.4 10.2 %fusion.10 = bf16[1024,512]{0,1:T(8,128)(2,1)} fusion(bf16[4096,512]{1,0:T(8,128)(2,1)} %all-gather.17.cloned.1.call-done, bf16[1024,4096]{1,0:T(8,128)(2,1)} %all-gather.11.cloned.1.call-done), kind=kOutput, calls=%fused_computation.16 | convolution fusion | flops 4295491584 | bytes 13631488 | tf_op jit(solution)/shard_map/jk,kqi->jqi/dot_general | solution.py:42
  469.6 0.0 all-gather.19.cloned.1.call-update
  469.6 0.1 reshape.273
  469.8 0.3 convolution_convert_fusion.1
  470.1 1.2 copy.24
  471.3 3.7 all-to-all-start
  475.0 9.7 %all-to-all-done = bf16[8,4,8192]{2,1,0:T(4,128)(2,1)S(1)} async-done(((bf16[8,4,8192]{2,1,0:T(4,128)(2,1)}), bf16[8,4,8192]{2,1,0:T(4,128)(2,1)S(1)}, u32[]{:S(2)}, u32[]{:S(2)}) %all-to-all-start) | async-done | bytes 524320 | tf_op jit(solution)/shard_map/all_to_all | solution.py:103
  484.7 0.4 fusion.1
  485.1 0.1 reshape.268
  485.3 0.2 copy.30
  485.4 2.0 all-gather.15.cloned.1.call-done
  487.5 55.8 %all-gather.19.cloned.1.call-done = bf16[1024,4096]{0,1:T(8,128)(2,1)} async-done(((bf16[1024,512]{0,1:T(8,128)(2,1)}), bf16[1024,4096]{0,1:T(8,128)(2,1)}) %all-gather.19.cloned.1.call-update) | async-done | bytes 8388624 | tf_op jit(solution)/shard_map/all_gather | solution.py:113
  543.3 6.0 %fusion.12 = f32[128]{0:T(128)S(1)} fusion(f32[1,128,1024]{1,2,0:T(8,128)S(1)} %copy.30, bf16[1024,4096]{0,1:T(8,128)(2,1)} %all-gather.19.cloned.1.call-done, bf16[128,4096]{1,0:T(8,128)(2,1)} %all-gather.15.cloned.1.call-done), kind=kOutput, calls=%fused_computation.19 | convolution fusion | flops 1074003840 | bytes 9961984 | tf_op jit(solution)/shard_map/tn,jqn->qtj/dot_general | solution.py:110
  549.3 0.1 reshape.266
  549.4 11.8 %psum.7 = f32[1,16,8]{2,1,0:T(8,128)S(1)} all-reduce(f32[1,16,8]{2,1,0:T(8,128)S(1)} %reshape.266), channel_id=1, replica_groups=mesh['tensor'=4,'example'=8] {'tensor'}, use_global_device_ids=true, to_apply=%region_7.8 | all-reduce | flops 128 | bytes 1024 | tf_op jit(solution)/shard_map/psum | solution.py:117
  561.2 0.1 fusion.18
  561.3 0.7 copy.31
  (10 shorter events, 0.1 us)
Async XLA Ops:
  6.5 85.9 %copy-start = (bf16[1,512,1024]{2,1,0:T(8,128)(2,1)S(1)}, bf16[1,512,1024]{2,1,0:T(8,128)(2,1)}, u32[]{:S(2)}) copy-start(bf16[1,512,1024]{2,1,0:T(8,128)(2,1)} %param.9) | copy-start | bytes 3145732
  6.5 85.9 %all-gather.9.cloned.1.call-start = ((), (), s32[]{:S(2)}) async-start(), calls=%async_computation.4 | async-start | bytes 5242880 | tf_op jit(solution)/shard_map/all_gather | solution.py:12
  7.3 141.6 %all-gather.11.cloned.1.call-start = ((), (), s32[]{:S(2)}) async-start(), calls=%async_computation.6 | async-start | bytes 9437184 | tf_op jit(solution)/shard_map/all_gather | solution.py:13
  8.0 215.6 %reduce-scatter.3.cloned.1.call-start = ((), (), s32[]{:S(2)}) async-start(), calls=%async_computation.5 | async-start | bytes 9437184 | tf_op jit(solution)/shard_map/reduce_scatter | solution.py:16
  101.4 209.3 %reduce-scatter.5.cloned.1.call-start = ((), (), s32[]{:S(2)}) async-start(), calls=%async_computation.7 | async-start | bytes 5242880 | tf_op jit(solution)/shard_map/reduce_scatter | solution.py:25
  233.8 134.6 %all-gather.13.cloned.1.call-start = ((), (), s32[]{:S(2)}) async-start(), calls=%async_computation.8 | async-start | bytes 9437184 | tf_op jit(solution)/shard_map/all_gather | solution.py:37
  313.4 65.1 %copy-start.1 = (bf16[16,8,1024]{2,1,0:T(8,128)(2,1)S(1)}, bf16[16,8,1024]{2,1,0:T(8,128)(2,1)}, u32[]{:S(2)}) copy-start(bf16[16,8,1024]{2,1,0:T(8,128)(2,1)} %param.14) | copy-start | bytes 786436
  313.4 65.3 %copy-start.3 = (s32[8,16]{1,0:T(8,128)S(1)}, s32[8,16]{1,0:T(8,128)}, u32[]{:S(2)}) copy-start(s32[8,16]{1,0:T(8,128)} %param.16) | copy-start | bytes 1540
  313.4 65.3 %copy-start.4 = (s32[128]{0:T(128)S(1)}, s32[128]{0:T(128)}, u32[]{:S(2)}) copy-start(s32[128]{0:T(128)} %param.17) | copy-start | bytes 1540
  313.4 65.3 %copy-start.5 = (s32[128]{0:T(128)S(1)}, s32[128]{0:T(128)}, u32[]{:S(2)}) copy-start(s32[128]{0:T(128)} %param.15) | copy-start | bytes 1540
  313.4 146.0 %all-gather.17.cloned.1.call-start = ((), (), s32[]{:S(2)}) async-start(), calls=%async_computation.10 | async-start | bytes 5242880 | tf_op jit(solution)/shard_map/all_gather | solution.py:45
  381.2 13.2 %all-to-all-start.1 = ((bf16[8,4,8192]{2,1,0:T(4,128)(2,1)}), bf16[8,4,8192]{2,1,0:T(4,128)(2,1)S(1)}, u32[]{:S(2)}, u32[]{:S(2)}) async-start(bf16[8,4,8192]{2,1,0:T(4,128)(2,1)} %copy.28), calls=%async_computation.3 | async-start | bytes 1048576 | tf_op jit(solution)/shard_map/all_to_all | solution.py:104
  384.7 102.8 %all-gather.15.cloned.1.call-start = ((), (), s32[]{:S(2)}) async-start(), calls=%async_computation.9 | async-start | bytes 1310720 | tf_op jit(solution)/shard_map/all_gather | solution.py:108
  395.7 74.0 %copy-start.2 = (bf16[16,8,1024]{2,1,0:T(8,128)(2,1)S(1)}, bf16[16,8,1024]{2,1,0:T(8,128)(2,1)}, u32[]{:S(2)}) copy-start(bf16[16,8,1024]{2,1,0:T(8,128)(2,1)} %param.13) | copy-start | bytes 786436
  395.7 147.6 %all-gather.19.cloned.1.call-start = ((), (), s32[]{:S(2)}) async-start(), calls=%async_computation.11 | async-start | bytes 9437184 | tf_op jit(solution)/shard_map/all_gather | solution.py:113
  471.3 13.4 %all-to-all-start = ((bf16[8,4,8192]{2,1,0:T(4,128)(2,1)}), bf16[8,4,8192]{2,1,0:T(4,128)(2,1)S(1)}, u32[]{:S(2)}, u32[]{:S(2)}) async-start(bf16[8,4,8192]{2,1,0:T(4,128)(2,1)} %copy.24), calls=%async_computation | async-start | bytes 1048576 | tf_op jit(solution)/shard_map/all_to_all | solution.py:103
Sparse Core Ops, SparseCore 0:
  8.9 83.4 all-gather.8
  94.3 54.4 all-gather.10
  152.3 71.2 reduce-scatter.2
  233.9 76.7 reduce-scatter.4
  313.5 54.8 all-gather.12
  378.6 80.7 all-gather.16
  461.0 26.4 all-gather.14
  489.4 53.8 all-gather.18
where the time goes:
time: 569 us
  waiting for transfers between devices  478 us (84%)
  matrix products  46.8 us (8%)
  between operations  13.7 us (2%)
  blocking collectives  11.8 us (2%)
  starting transfers between devices  7.87 us (1%)
  local copies, waits for them, and re-layouts  6.58 us (1%)
    all_gather x1, waiting for transfers between devices, body(): out_rows = lax.all_gather(basis_out, 'tensor', axis=1, tiled=True)  84.4 us
    reduce_scatter x1, waiting for transfers between devices, body(): lax.psum_scatter(jnp.einsum('kj,iqk->jqi', columns, rotated, preferred_el...  74.9 us
    reduce_scatter x1, waiting for transfers between devices, body(): lax.psum_scatter(jnp.einsum('ki,qkj->iqj', columns, queries, preferred_el...  74.8 us
    all_gather x1, waiting for transfers between devices, body(): lax.all_gather(turned, 'tensor', axis=0, tiled=True)  63.5 us
    all_gather x1, waiting for transfers between devices, body(): lax.all_gather(precond, 'example', axis=2, tiled=True)  55.8 us
    all_gather x1, waiting for transfers between devices, body(): lax.all_gather(scaled, 'example', axis=2, tiled=True)  54.8 us
    all_gather x1, waiting for transfers between devices, body(): in_rows = lax.all_gather(basis_in, 'example', axis=1, tiled=True)  47.3 us
    psum x1, blocking collectives, body(): lax.psum(partial_scores, 'tensor').reshape(query_total, list_len, token_len)  11.8 us
  transfers between devices with their start and end apart: 10, of which 10 were waited for; matrix products, arithmetic and copies ran while one was open for 5% of the time, Pallas kernels for 0%

commit v1 on v0

--- a/solution.py
+++ b/solution.py
@@ -2,6 +2,26 @@
 import jax.numpy as jnp
 from jax import lax
 from jax.sharding import PartitionSpec as P
+
+
+def _store_runs(xin, axis_key):
+    chunks = []
+    dev_n = jax.lax.axis_size(axis_key)
+    for k0 in [*range(dev_n)]:
+        chunks.append((k0, (k0 + 1) % dev_n))
+    copies = []
+    for k0 in [*range(dev_n)]:
+        copies.append((k0, (k0 - 1) % dev_n))
+    r_now, finding = ([xin], [xin])
+    for _ in range(dev_n // 2):
+        val = jax.lax.ppermute(r_now[-1], axis_name=axis_key, perm=chunks)
+        r_now.append(val)
+    for _ in [*range((dev_n - 1) // 2)]:
+        t1 = jax.lax.ppermute(finding[-1], axis_name=axis_key, perm=copies)
+        finding.append(t1)
+    v_next = jnp.concatenate([*r_now[::-1], *finding[1:]], axis=2)
+    mid_arr = jax.lax.axis_index(axis_key)
+    return jnp.roll(v_next, (mid_arr - dev_n // 2) * xin.shape[2], axis=2)
 
 
 def body(
@@ -33,10 +53,7 @@
     scaled = (core_sum / eigvals[:, None, :]).astype(jnp.bfloat16)
     columns = out_rows
     turned = jnp.einsum(
-        "jqk,ik->jqi",
-        lax.all_gather(scaled, "example", axis=2, tiled=True),
-        columns,
-        preferred_element_type=jnp.float32,
+        "jqk,ik->jqi", _store_runs(scaled, "example"), columns, preferred_element_type=jnp.float32
     ).astype(jnp.bfloat16)
     columns = in_rows
     precond = jnp.einsum(

time: 569 us -> 615 us (1.081)
  waiting for transfers between devices: 478 us -> 507 us
  local copies, waits for them, and re-layouts: 6.58 us -> 18.8 us
  starting transfers between devices: 7.87 us -> 15.7 us
    ppermute x0 -> x7, waiting for transfers between devices: none -> 85.2 us  [the longest x4 85.2 us: _store_runs(): val = jax.lax.ppermute(r_now[-1], axis_name=axis_key, perm=chunks)]
    all_gather x1 -> x0, waiting for transfers between devices: 54.8 us -> none  [body(): lax.all_gather(scaled, 'example', axis=2, tiled=True)]
    unnamed x13 -> x34, local copies, waits for them, and re-layouts: 1.96 us -> 12.8 us
    ppermute x0 -> x7, starting transfers between devices: none -> 7.99 us  [the longest x3 7.92 us: _store_runs(): t1 = jax.lax.ppermute(finding[-1], axis_name=axis_key, perm=copies)]
  transfers between devices with their start and end apart: 10 -> 16, of which waited for: 10 -> 13; matrix products, arithmetic and copies ran while one was open for 5% -> 5% of each run, Pallas kernels for 0% -> 0%
where the time goes in v1:
time: 615 us
  waiting for transfers between devices  507 us (82%)
  matrix products  44.6 us (7%)
  local copies, waits for them, and re-layouts  18.8 us (3%)
  starting transfers between devices  15.7 us (3%)
  between operations  13.8 us (2%)
  blocking collectives  11.8 us (2%)
    ppermute x4, waiting for transfers between devices, _store_runs(): val = jax.lax.ppermute(r_now[-1], axis_name=axis_key, perm=chunks)  85.2 us
    all_gather x1, waiting for transfers between devices, body(): out_rows = lax.all_gather(basis_out, 'tensor', axis=1, tiled=True)  84.4 us
    reduce_scatter x1, waiting for transfers between devices, body(): lax.psum_scatter(jnp.einsum('kj,iqk->jqi', columns, rotated, preferred_el...  74.9 us
    reduce_scatter x1, waiting for transfers between devices, body(): lax.psum_scatter(jnp.einsum('ki,qkj->iqj', columns, queries, preferred_el...  74.8 us
    all_gather x1, waiting for transfers between devices, body(): lax.all_gather(turned, 'tensor', axis=0, tiled=True)  62.1 us
    all_gather x1, waiting for transfers between devices, body(): lax.all_gather(precond, 'example', axis=2, tiled=True)  55.8 us
    all_gather x1, waiting for transfers between devices, body(): in_rows = lax.all_gather(basis_in, 'example', axis=1, tiled=True)  47.3 us
    unnamed x34, local copies, waits for them, and re-layouts  12.8 us
  transfers between devices with their start and end apart: 16, of which 13 were waited for; matrix products, arithmetic and copies ran while one was open for 5% of the time, Pallas kernels for 0%

profile of v1, /device:TPU:0, one launch (start us, length us, event | category | flops | bytes accessed | tf_op | source)
XLA Modules:
  0.0 614.6 jit_solution(9621458897676860353)
XLA Ops:
  6.5 0.7 all-gather.8.cloned.1.call-update
  7.3 0.7 all-gather.10.cloned.1.call-update
  8.1 84.4 %all-gather.8.cloned.1.call-done = bf16[512,4096]{1,0:T(8,128)(2,1)} async-done(((bf16[512,1024]{1,0:T(8,128)(2,1)}), bf16[512,4096]{1,0:T(8,128)(2,1)}) %all-gather.8.cloned.1.call-update) | async-done | bytes 4194320 | tf_op jit(solution)/shard_map/all_gather | solution.py:32
  92.4 9.0 %convert_bitcast_fusion = bf16[4096,1,1024]{2,0,1:T(8,128)(2,1)} fusion(bf16[512,4096]{1,0:T(8,128)(2,1)} %all-gather.8.cloned.1.call-done, bf16[1,512,1024]{2,1,0:T(8,128)(2,1)S(1)} %copy-done), kind=kOutput, calls=%fused_computation.10 | convolution fusion | flops 4299161600 | bytes 13631488 | tf_op jit(solution)/shard_map/ki,qkj->iqj/dot_general | solution.py:37
  101.5 47.3 %all-gather.10.cloned.1.call-done = bf16[1024,4096]{1,0:T(8,128)(2,1)} async-done(((bf16[1024,512]{1,0:T(8,128)(2,1)}), bf16[1024,4096]{1,0:T(8,128)(2,1)}) %all-gather.10.cloned.1.call-update) | async-done | bytes 8388624 | tf_op jit(solution)/shard_map/all_gather | solution.py:33
  148.8 74.8 %reduce-scatter.3.cloned.1.call-done = bf16[512,1,1024]{2,0,1:T(8,128)(2,1)} async-done(((bf16[4096,1,1024]{2,0,1:T(8,128)(2,1)}), bf16[512,1,1024]{2,0,1:T(8,128)(2,1)}) %reduce-scatter.3.cloned.1.call-update) | async-done | bytes 1048592 | tf_op jit(solution)/shard_map/reduce_scatter | solution.py:36
  223.6 10.2 %fusion.6 = bf16[4096,1,512]{0,2,1:T(8,128)(2,1)} fusion(bf16[1024,4096]{1,0:T(8,128)(2,1)} %all-gather.10.cloned.1.call-done, bf16[512,1,1024]{2,0,1:T(8,128)(2,1)} %reduce-scatter.3.cloned.1.call-done), kind=kOutput, calls=%fused_computation.12 | convolution fusion | flops 4297064448 | bytes 13631488 | tf_op jit(solution)/shard_map/kj,iqk->jqi/dot_general | solution.py:46
  233.9 1.9 copy.26
  235.8 74.9 %reduce-scatter.5.cloned.1.call-done = bf16[1024,1,512]{0,2,1:T(8,128)(2,1)} async-done(((bf16[4096,1,512]{0,2,1:T(8,128)(2,1)}), bf16[1024,1,512]{0,2,1:T(8,128)(2,1)}) %reduce-scatter.5.cloned.1.call-update) | async-done | bytes 1048592 | tf_op jit(solution)/shard_map/reduce_scatter | solution.py:45
  310.7 1.6 fusion.7
  312.4 0.1 collective-permute-start
  312.4 15.1 %collective-permute-done = bf16[1024,1,512]{0,2,1:T(8,128)(2,1)S(1)} collective-permute-done((bf16[1024,1,512]{0,2,1:T(8,128)(2,1)S(1)}, bf16[1024,1,512]{0,2,1:T(8,128)(2,1)S(1)}, u32[]{:S(2)}, u32[]{:S(2)}) %collective-permute-start) | collective-permute-done | bytes 1048608 | tf_op jit(solution)/shard_map/ppermute | solution.py:17
  327.6 2.6 collective-permute-start.4
  330.2 22.9 %collective-permute-done.1 = bf16[1024,1,512]{0,2,1:T(8,128)(2,1)S(1)} collective-permute-done((bf16[1024,1,512]{0,2,1:T(8,128)(2,1)S(1)}, bf16[1024,1,512]{0,2,1:T(8,128)(2,1)S(1)}, u32[]{:S(2)}, u32[]{:S(2)}) %collective-permute-start.1) | collective-permute-done | bytes 1048608 | tf_op jit(solution)/shard_map/ppermute | solution.py:17
  353.1 2.6 collective-permute-start.5
  355.7 23.6 %collective-permute-done.2 = bf16[1024,1,512]{0,2,1:T(8,128)(2,1)} collective-permute-done((bf16[1024,1,512]{0,2,1:T(8,128)(2,1)S(1)}, bf16[1024,1,512]{0,2,1:T(8,128)(2,1)}, u32[]{:S(2)}, u32[]{:S(2)}) %collective-permute-start.2) | collective-permute-done | bytes 1048608 | tf_op jit(solution)/shard_map/ppermute | solution.py:17
  379.3 2.6 collective-permute-start.6
  381.9 23.7 %collective-permute-done.3 = bf16[1024,1,512]{0,2,1:T(8,128)(2,1)} collective-permute-done((bf16[1024,1,512]{0,2,1:T(8,128)(2,1)}, bf16[1024,1,512]{0,2,1:T(8,128)(2,1)}, u32[]{:S(2)}, u32[]{:S(2)}) %collective-permute-start.3) | collective-permute-done | bytes 1048608 | tf_op jit(solution)/shard_map/ppermute | solution.py:17
  405.6 1.3 constant_dynamic-update-slice_fusion.15
  406.9 1.3 constant_dynamic-update-slice_fusion.14
  408.2 1.3 constant_dynamic-update-slice_fusion.13
  409.5 0.1 constant_dynamic-update-slice_fusion.12
  409.6 0.1 constant_dynamic-update-slice_fusion.11
  409.6 0.1 constant_dynamic-update-slice_fusion.10
  409.7 1.3 constant_dynamic-update-slice_fusion.9
  411.0 1.3 constant_dynamic-update-slice_fusion.8
  412.3 1.3 constant_dynamic-update-slice_fusion.7
  413.6 1.3 constant_dynamic-update-slice_fusion.6
  414.9 0.1 constant_dynamic-update-slice_fusion.5
  415.0 0.1 constant_dynamic-update-slice_fusion.4
  415.1 0.1 constant_dynamic-update-slice_fusion.3
  415.2 0.1 constant_dynamic-update-slice_fusion.2
  415.2 1.3 constant_dynamic-update-slice_fusion.1
  416.6 1.3 constant_dynamic-update-slice_fusion
  417.9 7.8 %fusion.8 = bf16[1024,512]{1,0:T(8,128)(2,1)} fusion(bf16[512,4096]{1,0:T(8,128)(2,1)} %all-gather.8.cloned.1.call-done, bf16[1024,1,8192]{0,2,1:T(8,128)(2,1)S(1)} %constant_dynamic-update-slice_fusion, s32[]{:T(128)S(6)} %select_n.62), kind=kOutput, calls=%fused_computation.15 | convolution fusion | flops 4295491584 | bytes 13631492 | tf_op jit(solution)/shard_map/jqk,ik->jqi/dot_general | solution.py:55
  425.7 0.1 reshape.275
  425.9 0.4 select_reduce_fusion.1
  426.4 0.3 convert_reduce_fusion.1
  426.7 0.1 iota_compare_fusion
  426.8 0.2 convert_reduce_fusion
  426.9 0.3 convolution_convert_fusion
  427.2 1.2 copy.28
  428.5 3.5 all-to-all-start.1
  432.1 9.6 %all-to-all-done.1 = bf16[8,4,8192]{2,1,0:T(4,128)(2,1)S(1)} async-done(((bf16[8,4,8192]{2,1,0:T(4,128)(2,1)}), bf16[8,4,8192]{2,1,0:T(4,128)(2,1)S(1)}, u32[]{:S(2)}, u32[]{:S(2)}) %all-to-all-start.1) | async-done | bytes 524320 | tf_op jit(solution)/shard_map/all_to_all | solution.py:121
  441.7 0.4 fusion.2
  442.1 0.8 reshape.265
  442.9 0.3 all-gather.16.cloned.1.call-start
  443.2 62.1 %all-gather.14.cloned.1.call-done = bf16[4096,512]{1,0:T(8,128)(2,1)} async-done(((bf16[1024,512]{1,0:T(8,128)(2,1)}), bf16[4096,512]{1,0:T(8,128)(2,1)}) %all-gather.14.cloned.1.call-update) | async-done | bytes 4194320 | tf_op jit(solution)/shard_map/all_gather | solution.py:62
  505.3 10.3 %fusion.11 = bf16[1024,512]{0,1:T(8,128)(2,1)} fusion(bf16[4096,512]{1,0:T(8,128)(2,1)} %all-gather.14.cloned.1.call-done, bf16[1024,4096]{1,0:T(8,128)(2,1)} %all-gather.10.cloned.1.call-done), kind=kOutput, calls=%fused_computation.17 | convolution fusion | flops 4295491584 | bytes 13631488 | tf_op jit(solution)/shard_map/jk,kqi->jqi/dot_general | solution.py:59
  515.6 0.1 reshape.273
  515.8 0.3 convolution_convert_fusion.1
  516.0 1.3 copy.24
  517.3 3.7 all-to-all-start
  521.0 9.7 %all-to-all-done = bf16[8,4,8192]{2,1,0:T(4,128)(2,1)S(1)} async-done(((bf16[8,4,8192]{2,1,0:T(4,128)(2,1)}), bf16[8,4,8192]{2,1,0:T(4,128)(2,1)S(1)}, u32[]{:S(2)}, u32[]{:S(2)}) %all-to-all-start) | async-done | bytes 524320 | tf_op jit(solution)/shard_map/all_to_all | solution.py:120
  530.8 0.4 fusion.1
  531.2 0.1 reshape.268
  531.3 0.2 copy.30
  531.5 1.8 all-gather.12.cloned.1.call-done
  533.3 55.8 %all-gather.16.cloned.1.call-done = bf16[1024,4096]{0,1:T(8,128)(2,1)} async-done(((bf16[1024,512]{0,1:T(8,128)(2,1)}), bf16[1024,4096]{0,1:T(8,128)(2,1)}) %all-gather.16.cloned.1.call-update) | async-done | bytes 8388624 | tf_op jit(solution)/shard_map/all_gather | solution.py:130
  589.1 6.0 fusion.13
  595.1 0.1 reshape.266
  595.1 11.8 %psum.7 = f32[1,16,8]{2,1,0:T(8,128)S(1)} all-reduce(f32[1,16,8]{2,1,0:T(8,128)S(1)} %reshape.266), channel_id=1, replica_groups=mesh['tensor'=4,'example'=8] {'tensor'}, use_global_device_ids=true, to_apply=%region_7.8 | all-reduce | flops 128 | bytes 1024 | tf_op jit(solution)/shard_map/psum | solution.py:134
  607.0 0.1 fusion.19
  607.1 0.7 copy.31
  (43 shorter events, 0.4 us)
Async XLA Ops:
  6.5 85.9 %copy-start = (bf16[1,512,1024]{2,1,0:T(8,128)(2,1)S(1)}, bf16[1,512,1024]{2,1,0:T(8,128)(2,1)}, u32[]{:S(2)}) copy-start(bf16[1,512,1024]{2,1,0:T(8,128)(2,1)} %param.9) | copy-start | bytes 3145732
  6.5 85.9 %all-gather.8.cloned.1.call-start = ((), (), s32[]{:S(2)}) async-start(), calls=%async_computation.4 | async-start | bytes 5242880 | tf_op jit(solution)/shard_map/all_gather | solution.py:32
  7.3 141.6 %all-gather.10.cloned.1.call-start = ((), (), s32[]{:S(2)}) async-start(), calls=%async_computation.6 | async-start | bytes 9437184 | tf_op jit(solution)/shard_map/all_gather | solution.py:33
  8.0 215.6 %reduce-scatter.3.cloned.1.call-start = ((), (), s32[]{:S(2)}) async-start(), calls=%async_computation.5 | async-start | bytes 9437184 | tf_op jit(solution)/shard_map/reduce_scatter | solution.py:36
  101.4 209.3 %reduce-scatter.5.cloned.1.call-start = ((), (), s32[]{:S(2)}) async-start(), calls=%async_computation.7 | async-start | bytes 5242880 | tf_op jit(solution)/shard_map/reduce_scatter | solution.py:45
  233.8 271.5 %all-gather.14.cloned.1.call-start = ((), (), s32[]{:S(2)}) async-start(), calls=%async_computation.9 | async-start | bytes 5242880 | tf_op jit(solution)/shard_map/all_gather | solution.py:62
  312.4 15.2 %collective-permute-start = (bf16[1024,1,512]{0,2,1:T(8,128)(2,1)S(1)}, bf16[1024,1,512]{0,2,1:T(8,128)(2,1)S(1)}, u32[]{:S(2)}, u32[]{:S(2)}) collective-permute-start(bf16[1024,1,512]{0,2,1:T(8,128)(2,1)S(1)} %fusion.7), channel_id=1, source_target_pairs={{0,1},{1,2},{2,3},{3,4},{4,5},{5,6},{6,7},{7,0},{8,9},{9,10},{10,1... | collective-permute-start | bytes 3145736 | tf_op jit(solution)/shard_map/ppermute | solution.py:17
  327.6 25.5 %collective-permute-start.1 = (bf16[1024,1,512]{0,2,1:T(8,128)(2,1)S(1)}, bf16[1024,1,512]{0,2,1:T(8,128)(2,1)S(1)}, u32[]{:S(2)}, u32[]{:S(2)}) collective-permute-start(bf16[1024,1,512]{0,2,1:T(8,128)(2,1)S(1)} %collective-permute-done), channel_id=1, source_target_pairs={{0,1},{1,2},{2,3},{3,4},{4,5},{5,6},{6,7},{7,0},{8,9},{9,10},{10,1... | collective-permute-start | bytes 3145736 | tf_op jit(solution)/shard_map/ppermute | solution.py:17
  327.6 25.5 %collective-permute-start.4 = (bf16[1024,1,512]{0,2,1:T(8,128)(2,1)S(1)}, bf16[1024,1,512]{0,2,1:T(8,128)(2,1)S(1)}, u32[]{:S(2)}, u32[]{:S(2)}) collective-permute-start(bf16[1024,1,512]{0,2,1:T(8,128)(2,1)S(1)} %fusion.7), channel_id=1, source_target_pairs={{0,7},{1,0},{2,1},{3,2},{4,3},{5,4},{6,5},{7,6},{8,15},{9,8},{10,9... | collective-permute-start | bytes 3145736 | tf_op jit(solution)/shard_map/ppermute | solution.py:20
  353.1 26.2 %copy-start.2 = (bf16[1024,1,512]{0,2,1:T(8,128)(2,1)}, bf16[1024,1,512]{0,2,1:T(8,128)(2,1)S(1)}, u32[]{:S(2)}) copy-start(bf16[1024,1,512]{0,2,1:T(8,128)(2,1)S(1)} %collective-permute-done.1) | copy-start | bytes 3145732
  353.1 26.2 %collective-permute-start.2 = (bf16[1024,1,512]{0,2,1:T(8,128)(2,1)S(1)}, bf16[1024,1,512]{0,2,1:T(8,128)(2,1)}, u32[]{:S(2)}, u32[]{:S(2)}) collective-permute-start(bf16[1024,1,512]{0,2,1:T(8,128)(2,1)S(1)} %collective-permute-done.1), channel_id=1, source_target_pairs={{0,1},{1,2},{2,3},{3,4},{4,5},{5,6},{6,7},{7,0},{8,9},{9,10},{10,1... | collective-permute-start | bytes 3145736 | tf_op jit(solution)/shard_map/ppermute | solution.py:17
  353.1 26.2 %collective-permute-start.5 = (bf16[1024,1,512]{0,2,1:T(8,128)(2,1)S(1)}, bf16[1024,1,512]{0,2,1:T(8,128)(2,1)}, u32[]{:S(2)}, u32[]{:S(2)}) collective-permute-start(bf16[1024,1,512]{0,2,1:T(8,128)(2,1)S(1)} %collective-permute-done.4), channel_id=1, source_target_pairs={{0,7},{1,0},{2,1},{3,2},{4,3},{5,4},{6,5},{7,6},{8,15},{9,8},{10,9... | collective-permute-start | bytes 3145736 | tf_op jit(solution)/shard_map/ppermute | solution.py:20
  379.3 26.3 %collective-permute-start.3 = (bf16[1024,1,512]{0,2,1:T(8,128)(2,1)}, bf16[1024,1,512]{0,2,1:T(8,128)(2,1)}, u32[]{:S(2)}, u32[]{:S(2)}) collective-permute-start(bf16[1024,1,512]{0,2,1:T(8,128)(2,1)} %collective-permute-done.2), channel_id=1, source_target_pairs={{0,1},{1,2},{2,3},{3,4},{4,5},{5,6},{6,7},{7,0},{8,9},{9,10},{10,1... | collective-permute-start | bytes 3145736 | tf_op jit(solution)/shard_map/ppermute | solution.py:17
  379.3 31.7 %collective-permute-start.6 = (bf16[1024,1,512]{0,2,1:T(8,128)(2,1)}, bf16[1024,1,512]{0,2,1:T(8,128)(2,1)}, u32[]{:S(2)}, u32[]{:S(2)}) collective-permute-start(bf16[1024,1,512]{0,2,1:T(8,128)(2,1)} %collective-permute-done.5), channel_id=1, source_target_pairs={{0,7},{1,0},{2,1},{3,2},{4,3},{5,4},{6,5},{7,6},{8,15},{9,8},{10,9... | collective-permute-start | bytes 3145736 | tf_op jit(solution)/shard_map/ppermute | solution.py:20
  381.9 33.0 %copy-start.3 = (bf16[1024,1,512]{0,2,1:T(8,128)(2,1)S(1)}, bf16[1024,1,512]{0,2,1:T(8,128)(2,1)}, u32[]{:S(2)}) copy-start(bf16[1024,1,512]{0,2,1:T(8,128)(2,1)} %copy-done.2) | copy-start | bytes 3145732
  416.5 9.2 %copy-start.4 = (bf16[16,8,1024]{2,1,0:T(8,128)(2,1)S(1)}, bf16[16,8,1024]{2,1,0:T(8,128)(2,1)}, u32[]{:S(2)}) copy-start(bf16[16,8,1024]{2,1,0:T(8,128)(2,1)} %param.14) | copy-start | bytes 786436
  416.6 9.3 %copy-start.6 = (s32[8,16]{1,0:T(8,128)S(1)}, s32[8,16]{1,0:T(8,128)}, u32[]{:S(2)}) copy-start(s32[8,16]{1,0:T(8,128)} %param.16) | copy-start | bytes 1540
  416.6 9.3 %copy-start.7 = (s32[128]{0:T(128)S(1)}, s32[128]{0:T(128)}, u32[]{:S(2)}) copy-start(s32[128]{0:T(128)} %param.17) | copy-start | bytes 1540
  416.6 9.3 %copy-start.8 = (s32[128]{0:T(128)S(1)}, s32[128]{0:T(128)}, u32[]{:S(2)}) copy-start(s32[128]{0:T(128)} %param.15) | copy-start | bytes 1540
  428.5 13.2 %all-to-all-start.1 = ((bf16[8,4,8192]{2,1,0:T(4,128)(2,1)}), bf16[8,4,8192]{2,1,0:T(4,128)(2,1)S(1)}, u32[]{:S(2)}, u32[]{:S(2)}) async-start(bf16[8,4,8192]{2,1,0:T(4,128)(2,1)} %copy.28), calls=%async_computation.3 | async-start | bytes 1048576 | tf_op jit(solution)/shard_map/all_to_all | solution.py:121
  432.0 83.7 %copy-start.5 = (bf16[16,8,1024]{2,1,0:T(8,128)(2,1)S(1)}, bf16[16,8,1024]{2,1,0:T(8,128)(2,1)}, u32[]{:S(2)}) copy-start(bf16[16,8,1024]{2,1,0:T(8,128)(2,1)} %param.13) | copy-start | bytes 786436
  432.0 101.3 %all-gather.12.cloned.1.call-start = ((), (), s32[]{:S(2)}) async-start(), calls=%async_computation.8 | async-start | bytes 1310720 | tf_op jit(solution)/shard_map/all_gather | solution.py:125
  442.9 146.1 %all-gather.16.cloned.1.call-start = ((), (), s32[]{:S(2)}) async-start(), calls=%async_computation.10 | async-start | bytes 9437184 | tf_op jit(solution)/shard_map/all_gather | solution.py:130
  505.3 102.4 %copy-start.1 = (bf16[1,512,1024]{2,1,0:T(8,128)(2,1)S(1)}, bf16[1,512,1024]{2,1,0:T(8,128)(2,1)}, u32[]{:S(2)}) copy-start(bf16[1,512,1024]{2,1,0:T(8,128)(2,1)} %param.9) | copy-start | bytes 3145732
  517.3 13.4 %all-to-all-start = ((bf16[8,4,8192]{2,1,0:T(4,128)(2,1)}), bf16[8,4,8192]{2,1,0:T(4,128)(2,1)S(1)}, u32[]{:S(2)}, u32[]{:S(2)}) async-start(bf16[8,4,8192]{2,1,0:T(4,128)(2,1)} %copy.24), calls=%async_computation | async-start | bytes 1048576 | tf_op jit(solution)/shard_map/all_to_all | solution.py:120
Sparse Core Ops, SparseCore 0:
  8.9 83.4 all-gather.7
  94.3 54.4 all-gather.9
  152.3 71.2 reduce-scatter.2
  233.9 76.7 reduce-scatter.4
  425.9 79.4 all-gather.13
  506.8 26.4 all-gather.11
  535.1 53.8 all-gather.15
